TPU v7x, 32 devices: a whole 2x2x4 slice. The times are simulated.
32 devices in a mesh: dp: 16 (over z, y, x), head: 2 (over core).
Axes of the slice: x: 2, y: 2, z: 4, core: 2. Of those that a mesh axis runs over, the one named last changes fastest.
Arguments:
- layer_in: float32 [4096, 768], P(('dp', 'head')), may hold values from -6 to 6
- grad_out: float32 [4096, 768], P(('dp', 'head')), may hold values from -6 to 6
- w_qkv: bfloat16 [3, 768, 768], P(None, None, 'head'), may hold values from -0.21875 to 0.21875
- w_attn: bfloat16 [768, 768], P('head'), may hold values from -3 to 3
- gain_attn: float32 [768], replicated, may hold values from 0.1 to 1.9
- shift_attn: float32 [768], replicated, may hold values from -3 to 3
- gain_moe: float32 [768], replicated, may hold values from 0.1 to 1.9
- shift_moe: float32 [768], replicated, may hold values from -3 to 3
- w_router: bfloat16 [768, 32], replicated, may hold values from -0.4375 to 0.4375
- w_in: bfloat16 [32, 768, 3072], P(('dp', 'head')), may hold values from -0.21875 to 0.21875
- w_hidden: bfloat16 [32, 3072, 768], P(('dp', 'head')), may hold values from -0.109375 to 0.109375
- expert_ids: int32 [4096, 2], P(('dp', 'head')), may hold values from 0 to 31, all different within a row; in each aligned block of 128 rows (0 to 127, 128 to 255, ...) at most 12 rows name the same one
- group_ids: int32 [16], P('dp'), may hold values from 0 to 1, as said below
- frozen: int32 [32], P(('dp', 'head')), may hold values from 0 to 1, as said below
Outputs:
- layer_out: float32 [4096, 768], P(('dp', 'head'))
- grad_in: float32 [4096, 768], P(('dp', 'head'))
- grad_qkv: float32 [3, 768, 768], P(None, 'dp', 'head')
- grad_attn: float32 [12, 49152], P('head', 'dp')
- grad_gain_attn: float32 [768], P(('dp', 'head'))
- grad_shift_attn: float32 [768], P(('dp', 'head'))
- grad_gain_moe: float32 [768], P(('dp', 'head'))
- grad_shift_moe: float32 [768], P(('dp', 'head'))
- grad_router: float32 [768, 32], P(('dp', 'head'))
- grad_w_in: float32 [32, 768, 3072], P(('dp', 'head'))
- grad_w_hidden: float32 [32, 3072, 768], P(('dp', 'head'))
Inputs may be any that keep to these rules, and one draw needn't show every extreme that they name: `expert_ids`: each row names two different experts. Among the 128 rows of one device no expert is named more than 12 times, a bound that some block reaches. `group_ids`: exactly half of the entries are 1. `frozen`: exactly half of the entries are 1.
All inputs are finite; a program needn't handle non-finite values.
Results may differ from a plain program's by a relative error of at most 0.012.
The roundings to bfloat16 on the way count: a program that leaves them out, or rounds other values in their place, can miss the bound.
Values may be sent and summed in bfloat16 or wider, within the bound.
A program may use at most 128 MiB of HBM per device.

v0:
```python
import jax
import jax.numpy as jnp
from jax import lax
from jax.sharding import PartitionSpec as P

HEAD_DIM = 64


norm_epsilon = 1e-05
masked_value = -1e30


def in_blocks(x, dim, size):
    before, after = (x.shape[:dim], x.shape[dim + 1 :])
    return jnp.moveaxis(x.reshape(*before, size, -1, *after), dim, 0)


def sum_at_owner(x, axis, dim):
    blocks = in_blocks(x, dim, lax.axis_size(axis))
    arrived = lax.all_to_all(blocks, axis, split_axis=0, concat_axis=0, tiled=True)
    return arrived.astype(jnp.float32).sum(axis=0)


def layer_norm(values, gain_vec, shift_vec):
    center = values - jnp.mean(values, axis=-1, keepdims=True)
    spread = jnp.mean(center * center, axis=-1, keepdims=True)
    return center * lax.rsqrt(spread + norm_epsilon) * gain_vec + shift_vec


def causal_mask(offset, q_rows, length, long_flag):
    q_pos = offset + jnp.arange(q_rows)
    k_pos = jnp.arange(length)
    half_len = length // 2
    same_doc = q_pos[:, None] // half_len == k_pos[None, :] // half_len
    return (k_pos[None, :] <= q_pos[:, None]) & (same_doc | (long_flag == 1))


def body(
    layer_in,
    grad_out,
    w_qkv,
    w_attn,
    gain_attn,
    shift_attn,
    gain_moe,
    shift_moe,
    w_router,
    w_in,
    w_hidden,
    expert_ids,
    group_ids,
    frozen,
):
    rows_dev = layer_in.shape[0]
    width = layer_in.shape[1]
    width_local = w_attn.shape[0]
    head_count = width_local // HEAD_DIM
    experts = w_router.shape[1]
    capacity = max(2, 3 * rows_dev // experts)
    long_flag = group_ids[0]
    score_scale = HEAD_DIM ** (-0.5)
    normed_attn, norm_attn_pull = jax.vjp(layer_norm, layer_in, gain_attn, shift_attn)
    normed_rows = lax.all_gather(normed_attn.astype(jnp.bfloat16), "head", axis=0, tiled=True)
    length = normed_rows.shape[0]
    q_rows = min(512, length)
    project = jnp.einsum(
        "rd,tdc->trc", normed_rows, w_qkv, preferred_element_type=jnp.float32
    ).astype(jnp.bfloat16)
    queries = project[0].reshape(length, head_count, HEAD_DIM)
    keys_all = project[1].reshape(length, head_count, HEAD_DIM)
    values_all = project[2].reshape(length, head_count, HEAD_DIM)

    def block_scores(offset):
        scores = (
            jnp.einsum("qhc,khc->hqk", queries, keys_all, preferred_element_type=jnp.float32)
            * score_scale
        )
        allowed = causal_mask(offset, q_rows, length, long_flag)
        return jnp.where(allowed[None], scores, masked_value)

    block_starts = list(range(0, length, q_rows))
    mixed_parts = []
    log_sums = []
    for offset in block_starts:
        scores = block_scores(offset)
        top_score = jnp.max(scores, axis=-1, keepdims=True)
        exp_scores = jnp.exp(scores - top_score)
        totals = jnp.sum(exp_scores, axis=-1, keepdims=True)
        probs = (exp_scores / totals).astype(jnp.bfloat16)
        log_sums.append(top_score + jnp.log(totals))
        mixed_parts.append(
            jnp.einsum("hqk,khc->qhc", probs, values_all, preferred_element_type=jnp.float32)
        )
    mixed_heads = mixed_parts[0].reshape(length, width_local).astype(jnp.bfloat16)
    attn_out = lax.psum_scatter(
        jnp.dot(mixed_heads, w_attn, preferred_element_type=jnp.float32),
        "head",
        scatter_dimension=0,
        tiled=True,
    )
    residual = layer_in + attn_out
    normed_moe, norm_moe_pull = jax.vjp(layer_norm, residual, gain_moe, shift_moe)
    moe_low = normed_moe.astype(jnp.bfloat16)
    logits = jnp.dot(moe_low, w_router, preferred_element_type=jnp.float32)
    selector = (expert_ids[:, :, None] == jnp.arange(experts)[None, None, :]).astype(jnp.float32)
    chosen = jnp.sum(logits[:, None, :] * selector, axis=-1)
    gate_probs = jax.nn.softmax(chosen, axis=-1)
    flat_ids = expert_ids.reshape(-1)
    one_hot = (flat_ids[:, None] == jnp.arange(experts)[None, :]).astype(jnp.int32)
    slot_ranks = jnp.sum((jnp.cumsum(one_hot, axis=0) - 1) * one_hot, axis=-1)
    slot_index = flat_ids * capacity + slot_ranks
    dispatch = (slot_index[:, None] == jnp.arange(experts * capacity)[None, :]).astype(jnp.bfloat16)
    dispatch = dispatch.reshape(rows_dev, expert_ids.shape[1], experts * capacity)
    send_rows = jnp.einsum("tkm,td->md", dispatch, moe_low, preferred_element_type=jnp.float32)
    send_rows = send_rows.astype(jnp.bfloat16).reshape(experts, capacity, width)
    w_first = w_in[0]
    w_second = w_hidden[0]
    slot_rows = lax.all_to_all(send_rows, ("dp", "head"), split_axis=0, concat_axis=0, tiled=True)
    hidden = jnp.einsum("sid,df->sif", slot_rows, w_first, preferred_element_type=jnp.float32)
    activated = jax.nn.gelu(hidden).astype(jnp.bfloat16)
    produced = jnp.einsum(
        "sif,fd->sid", activated, w_second, preferred_element_type=jnp.float32
    ).astype(jnp.bfloat16)
    produced, hidden, arrived = (produced, hidden, slot_rows)
    returned = lax.all_to_all(produced, ("dp", "head"), split_axis=0, concat_axis=0, tiled=True)
    picked = jnp.einsum(
        "tkm,md->tkd",
        dispatch,
        returned.reshape(experts * capacity, width),
        preferred_element_type=jnp.float32,
    )
    layer_out = residual + jnp.sum(gate_probs[:, :, None] * picked, axis=1)
    grad_gates = jnp.sum(picked * grad_out[:, None, :], axis=-1)
    grad_pair = (gate_probs[:, :, None] * grad_out[:, None, :]).astype(jnp.bfloat16)
    grad_slots = jnp.einsum("tkm,tkd->md", dispatch, grad_pair, preferred_element_type=jnp.float32)
    grad_slots = grad_slots.astype(jnp.bfloat16).reshape(experts, capacity, width)
    grad_arrived = lax.all_to_all(
        grad_slots, ("dp", "head"), split_axis=0, concat_axis=0, tiled=True
    )
    activated_full, gelu_pull = jax.vjp(jax.nn.gelu, hidden)
    activated = activated_full.astype(jnp.bfloat16)
    grad_act = jnp.einsum("sid,fd->sif", grad_arrived, w_second, preferred_element_type=jnp.float32)
    grad_hidden = gelu_pull(grad_act)[0].astype(jnp.bfloat16)
    trainable = (1 - frozen[0]).astype(jnp.float32)
    grad_w_hidden = (
        jnp.einsum("sif,sid->fd", activated, grad_arrived, preferred_element_type=jnp.float32)
        * trainable
    )[None]
    grad_w_in = (
        jnp.einsum("sid,sif->df", arrived, grad_hidden, preferred_element_type=jnp.float32)
        * trainable
    )[None]
    grad_rows = jnp.einsum(
        "sif,df->sid", grad_hidden, w_first, preferred_element_type=jnp.float32
    ).astype(jnp.bfloat16)
    grad_send = lax.all_to_all(grad_rows, ("dp", "head"), split_axis=0, concat_axis=0, tiled=True)
    grad_normed = jnp.einsum(
        "tkm,md->td",
        dispatch,
        grad_send.reshape(experts * capacity, width),
        preferred_element_type=jnp.float32,
    )
    grad_chosen = gate_probs * (
        grad_gates - jnp.sum(gate_probs * grad_gates, axis=-1, keepdims=True)
    )
    grad_logits = jnp.sum(selector * grad_chosen[:, :, None], axis=1).astype(jnp.bfloat16)
    grad_normed = grad_normed + jnp.einsum(
        "te,de->td", grad_logits, w_router, preferred_element_type=jnp.float32
    )
    grad_router = jnp.einsum("td,te->de", moe_low, grad_logits, preferred_element_type=jnp.float32)
    grad_resid_norm, grad_gain_moe, grad_shift_moe = norm_moe_pull(grad_normed)
    grad_resid = grad_out + grad_resid_norm
    grad_attn_rows = lax.all_gather(grad_resid.astype(jnp.bfloat16), "head", axis=0, tiled=True)
    grad_mixed = jnp.einsum("rd,cd->rc", grad_attn_rows, w_attn, preferred_element_type=jnp.float32)
    grad_mixed = grad_mixed.astype(jnp.bfloat16).reshape(length, head_count, HEAD_DIM)
    grad_w_attn = jnp.einsum(
        "rc,rd->cd", mixed_heads, grad_attn_rows, preferred_element_type=jnp.float32
    )
    grad_keys = jnp.zeros((length, head_count, HEAD_DIM), jnp.float32)
    grad_values = jnp.zeros((length, head_count, HEAD_DIM), jnp.float32)
    grad_query_parts = []
    for number, offset in enumerate(block_starts):
        scores = block_scores(offset)
        probs = jnp.exp(scores - log_sums[number])
        probs_low = probs.astype(jnp.bfloat16)
        grad_values = jnp.einsum(
            "hqk,qhc->khc", probs_low, grad_mixed, preferred_element_type=jnp.float32
        )
        grad_probs = jnp.einsum(
            "qhc,khc->hqk", grad_mixed, values_all, preferred_element_type=jnp.float32
        )
        grad_scores = probs * (grad_probs - jnp.sum(probs * grad_probs, axis=-1, keepdims=True))
        grad_scores = grad_scores.astype(jnp.bfloat16)
        grad_query_parts.append(
            jnp.einsum("hqk,khc->qhc", grad_scores, keys_all, preferred_element_type=jnp.float32)
            * score_scale
        )
        grad_keys = (
            jnp.einsum("hqk,qhc->khc", grad_scores, queries, preferred_element_type=jnp.float32)
            * score_scale
        )
    grad_queries = grad_query_parts[0]
    grad_project = (
        jnp.stack([grad_queries, grad_keys, grad_values])
        .reshape(3, length, width_local)
        .astype(jnp.bfloat16)
    )
    grad_w_qkv = jnp.einsum(
        "rd,trc->tdc", normed_rows, grad_project, preferred_element_type=jnp.float32
    )
    grad_normed_attn = lax.psum_scatter(
        jnp.einsum("trc,tdc->rd", grad_project, w_qkv, preferred_element_type=jnp.float32).astype(
            jnp.bfloat16
        ),
        "head",
        scatter_dimension=0,
        tiled=True,
    ).astype(jnp.float32)
    grad_input_norm, grad_gain_attn, grad_shift_attn = norm_attn_pull(grad_normed_attn)
    grad_in = grad_resid + grad_input_norm
    grad_qkv_sum, grad_attn_sum = (
        sum_at_owner(grad_w_qkv.astype(jnp.bfloat16), "dp", 1),
        sum_at_owner(
            grad_w_attn.reshape(head_count, HEAD_DIM * width).astype(jnp.bfloat16), "dp", 1
        ),
    )
    summed_small = (
        lax.psum_scatter(grad_gain_attn, ("dp", "head"), scatter_dimension=0, tiled=True),
        lax.psum_scatter(grad_shift_attn, ("dp", "head"), scatter_dimension=0, tiled=True),
        lax.psum_scatter(grad_gain_moe, ("dp", "head"), scatter_dimension=0, tiled=True),
        lax.psum_scatter(grad_shift_moe, ("dp", "head"), scatter_dimension=0, tiled=True),
        lax.psum_scatter(grad_router, ("dp", "head"), scatter_dimension=0, tiled=True),
    )
    return (
        layer_out,
        grad_in,
        grad_qkv_sum,
        grad_attn_sum,
        summed_small[0],
        summed_small[1],
        summed_small[2],
        summed_small[3],
        summed_small[4],
        grad_w_in,
        grad_w_hidden,
    )


def solution(mesh):
    placed = (
        P(("dp", "head"), None),
        P(("dp", "head"), None),
        P(None, None, "head"),
        P("head", None),
        P(),
        P(),
        P(),
        P(),
        P(),
        P(("dp", "head"), None, None),
        P(("dp", "head"), None, None),
        P(("dp", "head"), None),
        P("dp"),
        P(("dp", "head")),
    )
    return jax.shard_map(
        body,
        mesh=mesh,
        in_specs=placed,
        out_specs=(
            P(("dp", "head"), None),
            P(("dp", "head"), None),
            P(None, "dp", "head"),
            P("head", "dp"),
            P(("dp", "head")),
            P(("dp", "head")),
            P(("dp", "head")),
            P(("dp", "head")),
            P(("dp", "head"), None),
            P(("dp", "head"), None, None),
            P(("dp", "head"), None, None),
        ),
        check_vma=False,
    )
```

profile of v0, /device:TPU:0, one launch (start us, length us, event | category | flops | bytes accessed | tf_op | source)
XLA Modules:
  0.0 322.9 jit_solution(8029144456948712512)
XLA Ops:
  12.1 2.2 all_gather.6
  24.3 8.8 %reduce-scatter.6.cloned.1.call-done = f32[128,768]{1,0:T(8,128)} async-done(((f32[256,768]{1,0:T(8,128)}), f32[128,768]{1,0:T(8,128)}) %reduce-scatter.6.cloned.1.call-update) | async-done | bytes 393232 | tf_op jit(solution)/shard_map/reduce_scatter | solution.py:95
  35.9 2.1 fusion.74
  40.0 5.9 %all-to-all-start = ((bf16[32,12,768]{2,1,0:T(8,128)(2,1)}), bf16[32,12,768]{2,1,0:T(8,128)(2,1)}, u32[]{:S(2)}, u32[]{:S(2)}) async-start(bf16[32,12,768]{2,1,0:T(8,128)(2,1)} %reshape.397), calls=%async_computation.1 | async-start | bytes 1572864 | tf_op jit(solution)/shard_map/all_to_all | solution.py:118
  48.1 2.2 fusion.20
  52.3 14.2 %all-to-all-done = bf16[32,12,768]{2,1,0:T(8,128)(2,1)} async-done(((bf16[32,12,768]{2,1,0:T(8,128)(2,1)}), bf16[32,12,768]{2,1,0:T(8,128)(2,1)}, u32[]{:S(2)}, u32[]{:S(2)}) %all-to-all-start) | async-done | bytes 589856 | tf_op jit(solution)/shard_map/all_to_all | solution.py:118
  66.5 3.7 %all-to-all-start.2 = ((bf16[32,12,768]{2,1,0:T(8,128)(2,1)}), bf16[32,12,768]{2,1,0:T(8,128)(2,1)}, u32[]{:S(2)}, u32[]{:S(2)}) async-start(bf16[32,12,768]{2,1,0:T(8,128)(2,1)} %reshape.399), calls=%async_computation.3 | async-start | bytes 1572864 | tf_op jit(solution)/shard_map/all_to_all | solution.py:137
  70.2 4.6 %fusion.15 = f32[32,12,3072]{2,0,1:T(8,128)S(1)} fusion(bf16[1,768,3072]{2,1,0:T(8,128)(2,1)} %param.23, bf16[32,12,768]{2,1,0:T(8,128)(2,1)} %all-to-all-done), kind=kOutput, calls=%fused_computation.19 | convolution fusion | flops 1811939328 | bytes 10027008 | tf_op jit(solution)/shard_map/sid,df->sif/dot_general | solution.py:119
  74.9 6.9 %fusion.24 = bf16[32,12,768]{2,0,1:T(8,128)(2,1)S(1)} fusion(bf16[1,3072,768]{2,1,0:T(8,128)(2,1)} %param.24, f32[32,12,3072]{2,0,1:T(8,128)S(1)} %fusion.15), kind=kOutput, calls=%fused_computation.38 | convolution fusion | flops 1822851072 | bytes 10027008 | tf_op jit(solution)/shard_map/sif,fd->sid/dot_general | solution.py:121
  83.0 7.8 %all-to-all-done.2 = bf16[32,12,768]{2,1,0:T(8,128)(2,1)} async-done(((bf16[32,12,768]{2,1,0:T(8,128)(2,1)}), bf16[32,12,768]{2,1,0:T(8,128)(2,1)}, u32[]{:S(2)}, u32[]{:S(2)}) %all-to-all-start.2) | async-done | bytes 589856 | tf_op jit(solution)/shard_map/all_to_all | solution.py:137
  90.9 3.9 %all-to-all-start.1 = ((bf16[32,12,768]{2,1,0:T(8,128)(2,1)}), bf16[32,12,768]{2,1,0:T(8,128)(2,1)}, u32[]{:S(2)}, u32[]{:S(2)}) async-start(bf16[32,12,768]{2,1,0:T(8,128)(2,1)} %copy.141), calls=%async_computation.2 | async-start | bytes 1572864 | tf_op jit(solution)/shard_map/all_to_all | solution.py:125
  94.8 8.1 %fusion.8 = bf16[32,12,3072]{2,0,1:T(8,128)(2,1)S(1)} fusion(f32[32,12,3072]{2,0,1:T(8,128)} %copy-done.4, bf16[1,3072,768]{2,1,0:T(8,128)(2,1)} %param.24, bf16[32,12,768]{2,1,0:T(8,128)(2,1)} %all-to-all-done.2), kind=kOutput, calls=%fused_computation.12 | convolution fusion | flops 1835532288 | bytes 12386304 | tf_op jit(solution)/shard_map/sid,fd->sif/dot_general | solution.py:142
  102.9 5.2 %fusion.21 = bf16[32,12,768]{2,0,1:T(8,128)(2,1)S(1)} fusion(bf16[32,12,3072]{2,0,1:T(8,128)(2,1)S(1)} %fusion.8, bf16[1,768,3072]{2,1,0:T(8,128)(2,1)} %param.23), kind=kOutput, calls=%fused_computation.37 | convolution fusion | flops 1812234240 | bytes 7667712 | tf_op jit(solution)/shard_map/sif,df->sid/dot_general | solution.py:153
  109.5 5.7 %all-to-all-done.1 = bf16[32,12,768]{2,1,0:T(8,128)(2,1)} async-done(((bf16[32,12,768]{2,1,0:T(8,128)(2,1)}), bf16[32,12,768]{2,1,0:T(8,128)(2,1)}, u32[]{:S(2)}, u32[]{:S(2)}) %all-to-all-start.1) | async-done | bytes 589856 | tf_op jit(solution)/shard_map/all_to_all | solution.py:125
  115.2 3.7 %all-to-all-start.3 = ((bf16[32,12,768]{2,1,0:T(8,128)(2,1)}), bf16[32,12,768]{2,1,0:T(8,128)(2,1)}, u32[]{:S(2)}, u32[]{:S(2)}) async-start(bf16[32,12,768]{2,1,0:T(8,128)(2,1)} %copy.143), calls=%async_computation.4 | async-start | bytes 1572864 | tf_op jit(solution)/shard_map/all_to_all | solution.py:156
  119.6 2.0 reshape.406
  121.6 2.5 multiply_reduce_fusion.1
  124.2 15.4 %all-to-all-done.3 = bf16[32,12,768]{2,1,0:T(8,128)(2,1)} async-done(((bf16[32,12,768]{2,1,0:T(8,128)(2,1)}), bf16[32,12,768]{2,1,0:T(8,128)(2,1)}, u32[]{:S(2)}, u32[]{:S(2)}) %all-to-all-start.3) | async-done | bytes 589856 | tf_op jit(solution)/shard_map/all_to_all | solution.py:156
  148.9 2.1 all_gather.7
  155.4 3.1 multiply_reduce_fusion
  158.5 2.2 convert_element_type.136
  162.5 2.3 copy.173
  164.7 4.7 %all-to-all-start.5 = ((bf16[16,6,3072]{2,1,0:T(8,128)(2,1)}), bf16[16,6,3072]{2,1,0:T(8,128)(2,1)}, u32[]{:S(2)}, u32[]{:S(2)}) async-start(bf16[16,6,3072]{2,1,0:T(8,128)(2,1)} %bitcast.123), calls=%async_computation.7 | async-start | bytes 1572864 | tf_op jit(solution)/shard_map/all_to_all | solution.py:20
  175.8 3.0 convert_bitcast_fusion
  178.8 2.8 copy.152
  182.9 6.5 %all-to-all-done.5 = bf16[16,6,3072]{2,1,0:T(8,128)(2,1)} async-done(((bf16[16,6,3072]{2,1,0:T(8,128)(2,1)}), bf16[16,6,3072]{2,1,0:T(8,128)(2,1)}, u32[]{:S(2)}, u32[]{:S(2)}) %all-to-all-start.5) | async-done | bytes 589856 | tf_op jit(solution)/shard_map/all_to_all | solution.py:20
  189.5 5.0 %all-to-all-start.4 = ((bf16[16,3,48,384]{3,2,1,0:T(8,128)(2,1)}), bf16[16,3,48,384]{3,2,1,0:T(8,128)(2,1)}, u32[]{:S(2)}, u32[]{:S(2)}) async-start(bf16[16,3,48,384]{3,2,1,0:T(8,128)(2,1)} %copy.153), calls=%async_computation.6 | async-start | bytes 3538944 | tf_op jit(solution)/shard_map/all_to_all | solution.py:20
  194.6 9.5 %fusion = f32[1,3072,768]{2,1,0:T(8,128)} fusion(f32[]{:T(128)} %bitcast.29, bf16[32,12,768]{2,1,0:T(8,128)(2,1)} %all-to-all-done.2, f32[32,12,3072]{2,0,1:T(8,128)} %copy-done.4), kind=kOutput, calls=%fused_computation.1 | convolution fusion | flops 1824915456 | bytes 14745604 | tf_op jit(solution)/shard_map/sif,sid->fd/dot_general | solution.py:146
  205.8 8.5 %fusion.1 = f32[1,768,3072]{2,1,0:T(8,128)} fusion(bf16[32,12,3072]{2,0,1:T(8,128)(2,1)} %copy-done.57, f32[]{:T(128)} %bitcast.29, bf16[32,12,768]{2,1,0:T(8,128)(2,1)} %all-to-all-done), kind=kOutput, calls=%fused_computation.3 | convolution fusion | flops 1814298624 | bytes 12386308 | tf_op jit(solution)/shard_map/sid,sif->df/dot_general | solution.py:150
  217.7 43.1 %all-reduce.5 = (f32[768]{0:T(1024)S(1)}, f32[768]{0:T(1024)S(1)}, f32[768]{0:T(1024)S(1)}, f32[768]{0:T(1024)S(1)}) all-reduce(f32[768]{0:T(1024)S(1)} %get-tuple-element.15, f32[768]{0:T(1024)S(1)} %get-tuple-element.18, f32[768]{0:T(1024)S(1)} %copy-done.31, ...), channel_id=4, replica_groups=mesh['dp'=16,'head'=2] {'dp','head'}, use_global_device_ids=true, to_apply=%region_27.28.clone | all-reduce | flops 3072 | bytes 24576
  266.9 2.4 convert_reduce_fusion
  269.4 47.0 %reduce-scatter.10.cloned.1.call-done = f32[24,32]{1,0:T(8,128)} async-done(((f32[768,32]{1,0:T(8,128)}), f32[24,32]{1,0:T(8,128)}) %reduce-scatter.10.cloned.1.call-update) | async-done | bytes 3088
  (201 shorter events, 59.8 us)
Async XLA Ops:
  7.2 25.8 %reduce-scatter.6.cloned.1.call-start = ((), (), s32[]{:S(2)}) async-start(), calls=%async_computation.9 | async-start | bytes 1179648 | tf_op jit(solution)/shard_map/reduce_scatter | solution.py:95
  18.7 16.4 %copy-start.25 = (f32[768]{0:T(1024)S(1)}, f32[768]{0:T(1024)}, u32[]{:S(2)}) copy-start(f32[768]{0:T(1024)} %param.20) | copy-start | bytes 9220
  35.9 38.9 %copy-start.8 = (bf16[128,768]{1,0:T(8,128)(2,1)}, bf16[128,768]{1,0:T(8,128)(2,1)S(1)}, u32[]{:S(2)}) copy-start(bf16[128,768]{1,0:T(8,128)(2,1)S(1)} %add_convert_fusion) | copy-start | bytes 589828
  40.0 26.5 %all-to-all-start = ((bf16[32,12,768]{2,1,0:T(8,128)(2,1)}), bf16[32,12,768]{2,1,0:T(8,128)(2,1)}, u32[]{:S(2)}, u32[]{:S(2)}) async-start(bf16[32,12,768]{2,1,0:T(8,128)(2,1)} %reshape.397), calls=%async_computation.1 | async-start | bytes 1572864 | tf_op jit(solution)/shard_map/all_to_all | solution.py:118
  46.9 27.9 %copy-start.27 = (f32[128,2]{0,1:T(2,128)}, f32[128,2]{0,1:T(2,128)S(1)}, u32[]{:S(2)}) copy-start(f32[128,2]{0,1:T(2,128)S(1)} %select_reduce_fusion.1) | copy-start | bytes 3076
  46.9 27.9 %copy-start.37 = (f32[128]{0:T(128)}, f32[128]{0:T(128)S(1)}, u32[]{:S(2)}) copy-start(f32[128]{0:T(128)S(1)} %reduce_max.19) | copy-start | bytes 1540
  66.5 24.4 %all-to-all-start.2 = ((bf16[32,12,768]{2,1,0:T(8,128)(2,1)}), bf16[32,12,768]{2,1,0:T(8,128)(2,1)}, u32[]{:S(2)}, u32[]{:S(2)}) async-start(bf16[32,12,768]{2,1,0:T(8,128)(2,1)} %reshape.399), calls=%async_computation.3 | async-start | bytes 1572864 | tf_op jit(solution)/shard_map/all_to_all | solution.py:137
  90.9 24.4 %all-to-all-start.1 = ((bf16[32,12,768]{2,1,0:T(8,128)(2,1)}), bf16[32,12,768]{2,1,0:T(8,128)(2,1)}, u32[]{:S(2)}, u32[]{:S(2)}) async-start(bf16[32,12,768]{2,1,0:T(8,128)(2,1)} %copy.141), calls=%async_computation.2 | async-start | bytes 1572864 | tf_op jit(solution)/shard_map/all_to_all | solution.py:125
  102.9 16.7 %copy-start.30 = (f32[6,256]{1,0:T(8,128)S(1)}, f32[6,256]{1,0:T(8,128)}, u32[]{:S(2)}) copy-start(f32[6,256]{1,0:T(8,128)} %copy-done.29) | copy-start | bytes 18436
  102.9 18.8 %copy-start.40 = (s32[128,2]{0,1:T(2,128)S(1)}, s32[128,2]{0,1:T(2,128)}, u32[]{:S(2)}) copy-start(s32[128,2]{0,1:T(2,128)} %copy-done.39) | copy-start | bytes 3076
  102.9 18.8 %copy-start.50 = (f32[128,2]{0,1:T(2,128)S(1)}, f32[128,2]{0,1:T(2,128)}, u32[]{:S(2)}) copy-start(f32[128,2]{0,1:T(2,128)} %copy-done.49) | copy-start | bytes 3076
  108.2 16.0 %copy-start.28 = (f32[128,2]{0,1:T(2,128)S(1)}, f32[128,2]{0,1:T(2,128)}, u32[]{:S(2)}) copy-start(f32[128,2]{0,1:T(2,128)} %copy-done.27) | copy-start | bytes 3076
  108.2 16.0 %copy-start.38 = (f32[128]{0:T(128)S(1)}, f32[128]{0:T(128)}, u32[]{:S(2)}) copy-start(f32[128]{0:T(128)} %copy-done.37) | copy-start | bytes 1540
  108.2 16.0 %copy-start.44 = (f32[128]{0:T(128)S(1)}, f32[128]{0:T(128)}, u32[]{:S(2)}) copy-start(f32[128]{0:T(128)} %copy-done.43) | copy-start | bytes 1540
  108.2 16.0 %copy-start.34 = (s32[128,2]{0,1:T(2,128)S(1)}, s32[128,2]{0,1:T(2,128)}, u32[]{:S(2)}) copy-start(s32[128,2]{0,1:T(2,128)} %param.25) | copy-start | bytes 3076
  108.2 33.4 %copy-start.14 = (bf16[128,384]{0,1:T(8,128)(2,1)S(1)}, bf16[128,384]{0,1:T(8,128)(2,1)}, u32[]{:S(2)}) copy-start(bf16[128,384]{0,1:T(8,128)(2,1)} %convert_reduce_fusion.3) | copy-start | bytes 294916
  108.2 34.8 %copy-start.23 = (bf16[768,32]{0,1:T(8,128)(2,1)S(1)}, bf16[768,32]{0,1:T(8,128)(2,1)}, u32[]{:S(2)}) copy-start(bf16[768,32]{0,1:T(8,128)(2,1)} %param.22) | copy-start | bytes 147460
  108.2 34.8 %copy-start.26 = (f32[768]{0:T(1024)S(1)}, f32[768]{0:T(1024)}, u32[]{:S(2)}) copy-start(f32[768]{0:T(1024)} %param.20) | copy-start | bytes 9220
  108.2 34.8 %copy-start.42 = (f32[128]{0:T(128)S(1)}, f32[128]{0:T(128)}, u32[]{:S(2)}) copy-start(f32[128]{0:T(128)} %copy-done.41) | copy-start | bytes 1540
  108.3 34.8 %copy-start.48 = (f32[128]{0:T(128)S(1)}, f32[128]{0:T(128)}, u32[]{:S(2)}) copy-start(f32[128]{0:T(128)} %copy-done.47) | copy-start | bytes 1540
  108.3 36.7 %copy-start.56 = (f32[128]{0:T(128)S(1)}, f32[128]{0:T(128)}, u32[]{:S(2)}) copy-start(f32[128]{0:T(128)} %copy-done.55) | copy-start | bytes 1540
  115.2 24.4 %all-to-all-start.3 = ((bf16[32,12,768]{2,1,0:T(8,128)(2,1)}), bf16[32,12,768]{2,1,0:T(8,128)(2,1)}, u32[]{:S(2)}, u32[]{:S(2)}) async-start(bf16[32,12,768]{2,1,0:T(8,128)(2,1)} %copy.143), calls=%async_computation.4 | async-start | bytes 1572864 | tf_op jit(solution)/shard_map/all_to_all | solution.py:156
  160.7 12.7 %copy-start.13 = (bf16[1,256,384]{1,2,0:T(8,128)(2,1)S(1)}, bf16[1,256,384]{1,2,0:T(8,128)(2,1)}, u32[]{:S(2)}) copy-start(bf16[1,256,384]{1,2,0:T(8,128)(2,1)} %copy-done.12) | copy-start | bytes 589828
  164.7 24.8 %all-to-all-start.5 = ((bf16[16,6,3072]{2,1,0:T(8,128)(2,1)}), bf16[16,6,3072]{2,1,0:T(8,128)(2,1)}, u32[]{:S(2)}, u32[]{:S(2)}) async-start(bf16[16,6,3072]{2,1,0:T(8,128)(2,1)} %bitcast.123), calls=%async_computation.7 | async-start | bytes 1572864 | tf_op jit(solution)/shard_map/all_to_all | solution.py:20
  189.5 77.4 %all-to-all-start.4 = ((bf16[16,3,48,384]{3,2,1,0:T(8,128)(2,1)}), bf16[16,3,48,384]{3,2,1,0:T(8,128)(2,1)}, u32[]{:S(2)}, u32[]{:S(2)}) async-start(bf16[16,3,48,384]{3,2,1,0:T(8,128)(2,1)} %copy.153), calls=%async_computation.6 | async-start | bytes 3538944 | tf_op jit(solution)/shard_map/all_to_all | solution.py:20
  194.5 20.8 %reduce-scatter.8.cloned.1.call-start = ((), (), s32[]{:S(2)}) async-start(), calls=%async_computation.10 | async-start | bytes 589824 | tf_op jit(solution)/shard_map/reduce_scatter | solution.py:211
  205.7 12.0 %copy-start.31 = (f32[768]{0:T(1024)S(1)}, f32[768]{0:T(1024)}, u32[]{:S(2)}) copy-start(f32[768]{0:T(1024)} %get-tuple-element.11) | copy-start | bytes 9220
  205.7 12.0 %copy-start.32 = (f32[768]{0:T(1024)S(1)}, f32[768]{0:T(1024)}, u32[]{:S(2)}) copy-start(f32[768]{0:T(1024)} %get-tuple-element.17) | copy-start | bytes 9220
  205.7 57.4 %copy-start.5 = (f32[128,768]{1,0:T(8,128)S(1)}, f32[128,768]{1,0:T(8,128)}, u32[]{:S(2)}) copy-start(f32[128,768]{1,0:T(8,128)} %param.15) | copy-start | bytes 1179652
  205.7 57.4 %copy-start.7 = (f32[128,768]{1,0:T(8,128)S(1)}, f32[128,768]{1,0:T(8,128)}, u32[]{:S(2)}) copy-start(f32[128,768]{1,0:T(8,128)} %copy-done.6) | copy-start | bytes 1179652
  205.7 57.4 %copy-start.52 = (f32[128]{0:T(128)S(1)}, f32[128]{0:T(128)}, u32[]{:S(2)}) copy-start(f32[128]{0:T(128)} %copy-done.51) | copy-start | bytes 1540
  205.7 110.6 %reduce-scatter.10.cloned.1.call-start = ((), (), s32[]{:S(2)}) async-start(), calls=%async_computation.11 | async-start | bytes 405504
  (35 other events, 170.9 us)
Sparse Core Ops, SparseCore 0:
  22.1 10.8 reduce-scatter.5
  205.7 9.0 reduce-scatter.7
  220.3 95.9 reduce-scatter.9
where the time goes:
time: 325 us; the launch traced here: 323 us
  waiting for transfers between devices  105 us (32%)
  matrix products  73.2 us (23%)
  blocking collectives  47.3 us (15%)
  local copies, waits for them, and re-layouts  32.7 us (10%)
  starting transfers between devices  27 us (8%)
  other arithmetic  21.1 us (6%)
  between operations  16.1 us (5%)
    unnamed x4, waiting for transfers between devices  47 us
    unnamed x1, blocking collectives  43.1 us
    all_to_all x1, waiting for transfers between devices, body(): lax.all_to_all(grad_rows, ('dp', 'head'), split_axis=0, concat_axis=0, ti...  15.4 us
    all_to_all x1, waiting for transfers between devices, body(): lax.all_to_all(send_rows, ('dp', 'head'), split_axis=0, concat_axis=0, ti...  14.2 us
    all_to_all x2, starting transfers between devices, sum_at_owner(): lax.all_to_all(blocks, axis, split_axis=0, concat_axis=0, tiled=True)  9.68 us
    dot_general x1, matrix products, body(): jnp.einsum('sif,sid->fd', activated, grad_arrived, preferred_element_type...  9.53 us
    reduce_scatter x1, waiting for transfers between devices, body(): lax.psum_scatter(jnp.dot(mixed_heads, w_attn, preferred_element_type=jnp....  8.75 us
    dot_general x1, matrix products, body(): jnp.einsum('sid,sif->df', arrived, grad_hidden, preferred_element_type=jn...  8.48 us
  transfers between devices with their start and end apart: 9, of which 7 were waited for; matrix products, arithmetic and copies ran while one was open for 26% of the time, Pallas kernels for 0%

commit v1 on v0

--- a/solution.py
+++ b/solution.py
@@ -1,13 +1,808 @@
+import functools
+
 import jax
 import jax.numpy as jnp
 from jax import lax
+from jax.experimental import pallas as pl
+from jax.experimental.pallas import tpu as pltpu
 from jax.sharding import PartitionSpec as P
 
 HEAD_DIM = 64
-
-
 norm_epsilon = 1e-05
 masked_value = -1e30
+MESH = pl.DeviceIdType.MESH
+f32 = jnp.float32
+bf16 = jnp.bfloat16
+highest = lax.Precision.HIGHEST
+
+
+def mm(a, b, dims=((1,), (0,)), precision=None):
+    return lax.dot_general(a, b, (dims, ((), ())), precision=precision, preferred_element_type=f32)
+
+
+NN = ((1,), (0,))
+NT = ((1,), (1,))
+TN = ((0,), (0,))
+
+
+def iota(shape, dim):
+    return lax.broadcasted_iota(jnp.int32, shape, dim)
+
+
+def hat(x):
+    c = x - jnp.mean(x, axis=-1, keepdims=True)
+    r = lax.rsqrt(jnp.mean(c * c, axis=-1, keepdims=True) + norm_epsilon)
+    return c * r, r
+
+
+def norm_back(dy, x_hat, r, gain):
+    dyg = dy * gain
+    m1 = jnp.mean(dyg, axis=-1, keepdims=True)
+    m2 = jnp.mean(dyg * x_hat, axis=-1, keepdims=True)
+    return r * (dyg - m1 - x_hat * m2)
+
+
+def gelu_both(x):
+    k = 0.7978845608028654
+    x2 = x * x
+    t = jnp.tanh(k * (x + 0.044715 * x2 * x))
+    half = 0.5 * (1.0 + t)
+    slope = half + 0.5 * x * (1.0 - t * t) * (k * (1.0 + 0.134145 * x2))
+    return x * half, slope
+
+
+def layer_kernel(
+    n_dp,
+    n_head,
+    in_hbm,
+    gout_hbm,
+    wqkv_hbm,
+    wattn_hbm,
+    gain_attn,
+    shift_attn,
+    gain_moe,
+    shift_moe,
+    wr_ref,
+    win_hbm,
+    whid_hbm,
+    ids_ref,
+    group_ref,
+    lout_hbm,
+    gin_hbm,
+    rs_out_hbm,
+    small_hbm,
+    xs_hbm,
+    gp_hbm,
+    act_hbm,
+    gh_hbm,
+    x_in,
+    g_out,
+    wqkv,
+    wattn,
+    win,
+    whid,
+    nr,
+    qkv,
+    probs,
+    mixed,
+    apart,
+    arecv,
+    resid,
+    sel_a,
+    sel_b1,
+    sel_b2,
+    s_go,
+    r_go,
+    s_x,
+    r_x,
+    s_gt,
+    r_gt,
+    s_gr,
+    r_gr,
+    s_h,
+    r_h,
+    s_pr,
+    r_pr,
+    xs,
+    gos,
+    act,
+    gh,
+    grow,
+    gar,
+    gmix,
+    gqkv,
+    npart,
+    nrecv,
+    rsb,
+    rc0,
+    rc1,
+    rc2,
+    rc3,
+    rsf,
+    sm_s,
+    sm_r,
+    lout,
+    gin,
+    small,
+    ld_sem,
+    out_sem,
+    pair_s,
+    pair_r,
+    a2a_s,
+    a2a_r,
+    rs_s,
+    rs_r,
+    self_sem,
+):
+    n = n_dp * n_head
+    dp = lax.axis_index("dp")
+    hd = lax.axis_index("head")
+    me = dp * n_head + hd
+    rows, width = x_in.shape
+    length = nr.shape[0]
+    ff = act.shape[1]
+    experts = wr_ref.shape[1]
+    wl = wattn.shape[0]
+    half_w = width // 2
+    packed = s_x.shape[1]
+
+    def dev(p):
+        return (p // n_head, lax.rem(p, n_head))
+
+    loads = [
+        pltpu.make_async_copy(in_hbm, x_in, ld_sem.at[0]),
+        pltpu.make_async_copy(gout_hbm, g_out, ld_sem.at[1]),
+        pltpu.make_async_copy(wqkv_hbm, wqkv, ld_sem.at[2]),
+        pltpu.make_async_copy(wattn_hbm, wattn, ld_sem.at[3]),
+        pltpu.make_async_copy(win_hbm.at[0], win, ld_sem.at[4]),
+        pltpu.make_async_copy(whid_hbm.at[0], whid, ld_sem.at[5]),
+    ]
+    for c in loads:
+        c.start()
+    bar = pltpu.get_barrier_semaphore()
+
+    def greet(i, c):
+        p = lax.rem(me + i, n)
+        pl.semaphore_signal(bar, inc=1, device_id=dev(p), device_id_type=MESH)
+        return c
+
+    lax.fori_loop(1, n, greet, 0)
+
+    quarter = n // 4
+    z = me // quarter
+    far1 = (lax.rem(z + 2, 4) * quarter, quarter, 0)
+    far2 = ((3 - z) * quarter, quarter, 1)
+    near = ((z // 2) * 2 * quarter, 2 * quarter, 2)
+    order = (far1, far2, near)
+
+    def x_copy(ph, src, dst, unit, p, q):
+        if unit:
+            s = src.at[pl.ds(pl.multiple_of(p * unit, unit), unit)]
+            d = dst.at[pl.ds(pl.multiple_of(q * unit, unit), unit)]
+        else:
+            s = src.at[p]
+            d = dst.at[q]
+        return pltpu.make_async_remote_copy(
+            s, d, a2a_s.at[ph, p], a2a_r.at[ph, q], device_id=dev(p), device_id_type=MESH
+        )
+
+    def send_group(ph, src, dst, unit, group):
+        base, count, _ = group
+
+        def go(j, c):
+            p = base + lax.rem(me + j, count)
+
+            @pl.when(p != me)
+            def _():
+                x_copy(ph, src, dst, unit, p, me).start()
+
+            return c
+
+        lax.fori_loop(0, count, go, 0)
+
+    def wait_group(ph, src, dst, unit, group):
+        base, count, _ = group
+
+        def go(j, c):
+            p = base + lax.rem(me + j, count)
+
+            @pl.when(p != me)
+            def _():
+                x_copy(ph, src, dst, unit, p, p).wait_recv()
+
+            return c
+
+        lax.fori_loop(0, count, go, 0)
+
+    def drain(ph, src, dst, unit):
+        def go(i, c):
+            p = lax.rem(me + i, n)
+            x_copy(ph, src, dst, unit, p, me).wait_send()
+            return c
+
+        lax.fori_loop(1, n, go, 0)
+
+    def self_copy(ph, src, dst, unit):
+        if unit:
+            at = pl.ds(pl.multiple_of(me * unit, unit), unit)
+        else:
+            at = me
+        return pltpu.make_async_copy(src.at[at], dst.at[at], self_sem.at[ph])
+
+    def pair_copy(k, src, dst):
+        return pltpu.make_async_remote_copy(
+            src, dst, pair_s.at[k], pair_r.at[k], device_id=(dp, 1 - hd), device_id_type=MESH
+        )
+
+    mine = pl.ds(pl.multiple_of(hd * rows, rows), rows)
+    other = pl.ds(pl.multiple_of((1 - hd) * rows, rows), rows)
+
+    lane_e = iota((rows, experts), 1)
+    hits = [jnp.where(lane_e == ids_ref[:, k : k + 1], 1.0, 0.0) for k in range(2)]
+    below = jnp.where(iota((rows, rows), 0) > iota((rows, rows), 1), 1.0, 0.0).astype(bf16)
+    before = mm(below, (hits[0] + hits[1]).astype(bf16))
+    ranks = [jnp.sum(before * hits[k], axis=1, keepdims=True) for k in range(2)]
+    col = iota((rows, 8 * n), 1).astype(f32)
+    for k in range(2):
+        first = 8.0 * ids_ref[:, k : k + 1].astype(f32)
+        rk = ranks[k]
+        sel_a[k] = jnp.where((rk < 8.0) & (col == first + rk), 1.0, 0.0).astype(bf16)
+        sel_b1[k] = jnp.where((rk >= 8.0) & (col == first + rk - 8.0), 1.0, 0.0).astype(bf16)
+        sel_b2[k] = jnp.where((rk >= 8.0) & (col == first + rk - 4.0), 1.0, 0.0).astype(bf16)
+
+    def spread(block, dst):
+        dst[:, :width] = mm(sel_a[0] + sel_a[1], block, TN).astype(bf16)
+        dst[:, width:] = (
+            mm(sel_b1[0] + sel_b1[1], block[:, :half_w], TN)
+            + mm(sel_b2[0] + sel_b2[1], block[:, half_w:], TN)
+        ).astype(bf16)
+
+    def collect(src, k):
+        if k is None:
+            a, b1, b2 = (s[0] + s[1] for s in (sel_a, sel_b1, sel_b2))
+        else:
+            a, b1, b2 = sel_a[k], sel_b1[k], sel_b2[k]
+        tail = src[:, width:]
+        return mm(a, src[:, :width]) + jnp.concatenate([mm(b1, tail), mm(b2, tail)], axis=1)
+
+    loads[0].wait()
+    x_hat, _ = hat(x_in[...])
+    nr[mine] = (x_hat * gain_attn[...] + shift_attn[...]).astype(bf16)
+    loads[1].wait()
+    spread(g_out[...].astype(bf16), s_go)
+    pl.semaphore_wait(bar, n - 1)
+    gather = pair_copy(0, nr.at[mine], nr.at[mine])
+    gather.start()
+    for group in order:
+        send_group(0, s_go, r_go, 8, group)
+    self_copy(0, s_go, r_go, 8).start()
+
+    loads[2].wait()
+    gather.wait()
+    for t in range(3):
+        qkv[t] = mm(nr[...], wqkv[t]).astype(bf16)
+    long_flag = group_ref[0]
+    scale = HEAD_DIM ** (-0.5)
+    lane = iota((length, 2 * HEAD_DIM), 1)
+    lows = [lane < HEAD_DIM, lane >= HEAD_DIM]
+    q_pos = iota((length, length), 0)
+    k_pos = iota((length, length), 1)
+    same = (q_pos < length // 2) == (k_pos < length // 2)
+    bias = jnp.where(
+        (k_pos <= q_pos) & (same | (long_flag == 1)), 0.0, masked_value
+    )
+
+    def attend(j, c):
+        cols = pl.ds(pl.multiple_of(j * 128, 128), 128)
+        q, k, v = qkv[0, :, cols], qkv[1, :, cols], qkv[2, :, cols]
+        outs = []
+        for s in range(2):
+            sc = mm(jnp.where(lows[s], q, jnp.zeros_like(q)), k, NT) * scale
+            sc = jnp.where(bias == 0.0, sc, masked_value)
+            e = jnp.exp(sc - jnp.max(sc, axis=-1, keepdims=True))
+            p = e / jnp.sum(e, axis=-1, keepdims=True)
+            probs[2 * j + s] = p
+            outs.append(mm(p.astype(bf16), v))
+        mixed[:, cols] = jnp.where(lows[0], outs[0], outs[1]).astype(bf16)
+        return c
+
+    lax.fori_loop(0, wl // 128, attend, 0)
+    loads[3].wait()
+    apart[...] = mm(mixed[other, :], wattn[...])
+    half_sum = pair_copy(1, apart, arecv)
+    half_sum.start()
+    own = mm(mixed[mine, :], wattn[...]) + x_in[...]
+    half_sum.wait()
+    resid[...] = own + arecv[...]
+    y_hat, _ = hat(resid[...])
+    low = (y_hat * gain_moe[...] + shift_moe[...]).astype(bf16)
+    spread(low, s_x)
+    for group in order:
+        send_group(1, s_x, r_x, 8, group)
+    self_copy(1, s_x, r_x, 8).start()
+    logits = mm(low, wr_ref[...])
+    chosen = [jnp.sum(logits * hits[k], axis=1, keepdims=True) for k in range(2)]
+    top = jnp.maximum(chosen[0], chosen[1])
+    exps = [jnp.exp(c - top) for c in chosen]
+    gates = [e / (exps[0] + exps[1]) for e in exps]
+    lane128 = iota((rows, 128), 1).astype(f32)
+    marks = [jnp.where(lane128 == ranks[k], 1.0, 0.0) for k in range(2)]
+    s_gt[:, 0, :] = mm(hits[0], gates[0] * marks[0], TN, highest) + mm(
+        hits[1], gates[1] * marks[1], TN, highest
+    )
+    for group in order:
+        send_group(2, s_gt, r_gt, 0, group)
+    self_copy(2, s_gt, r_gt, 0).start()
+
+    loads[4].wait()
+    loads[5].wait()
+    fb = 512
+    starts = (0, 12 * quarter, 24 * quarter)
+    self_copy(0, s_go, r_go, 8).wait()
+    self_copy(1, s_x, r_x, 8).wait()
+    self_copy(2, s_gt, r_gt, 0).wait()
+    for base, count, which in (near, far1, far2):
+        group = (base, count, which)
+        m = 12 * count
+        at = starts[which]
+        for ph, s, d, u in ((0, s_go, r_go, 8), (2, s_gt, r_gt, 0), (1, s_x, r_x, 8)):
+            wait_group(ph, s, d, u, group)
+        blk = pl.ds(pl.multiple_of(base * 8, 8 * count), 8 * count)
+        r4 = iota((4 * count, 8 * count), 0)
+        c8 = iota((4 * count, 8 * count), 1)
+        hit = (r4 // 4) == (c8 // 8)
+        p1 = jnp.where(hit & ((r4 % 4) == (c8 % 8)), 1.0, 0.0).astype(bf16)
+        p2 = jnp.where(hit & ((r4 % 4) + 4 == (c8 % 8)), 1.0, 0.0).astype(bf16)
+        for src, dst in ((r_x, xs), (r_go, gos)):
+            dst[at : at + 8 * count] = src[blk, :width]
+            tail = src[blk, width:]
+            dst[at + 8 * count : at + m] = jnp.concatenate(
+                [mm(p1, tail).astype(bf16), mm(p2, tail).astype(bf16)], axis=1
+            )
+        rr = iota((m, count), 0)
+        source_of = jnp.where(rr < 8 * count, rr // 8, (rr - 8 * count) // 4)
+        e_of = jnp.where(source_of == iota((m, count), 1), 1.0, 0.0)
+        rl = iota((m, 128), 0)
+        lane_of = jnp.where(rl < 8 * count, rl % 8, 8 + (rl - 8 * count) % 4)
+        l_of = jnp.where(lane_of == iota((m, 128), 1), 1.0, 0.0)
+        gate = jnp.sum(
+            mm(e_of, r_gt[pl.ds(base, count), 0, :], NN, highest) * l_of, axis=1, keepdims=True
+        )
+        rows_m = slice(at, at + m)
+        gos[rows_m] = (gos[rows_m].astype(f32) * gate).astype(bf16)
+
+        def up(j, acc):
+            cols = pl.ds(pl.multiple_of(j * fb, fb), fb)
+            hidden = mm(xs[rows_m], win[:, cols])
+            a, slope = gelu_both(hidden)
+            a = a.astype(bf16)
+            act[rows_m, cols] = a
+            ga = mm(gos[rows_m], whid[cols, :], NT)
+            gh[rows_m, cols] = (slope * ga).astype(bf16)
+            prod = ga * a.astype(f32)
+            for q in range(fb // 128):
+                acc = acc + prod[:, 128 * q : 128 * q + 128]
+            return acc
+
+        dot_sum = lax.fori_loop(0, ff // fb, up, jnp.zeros((m, 128), f32))
+        dots = jnp.sum(dot_sum, axis=1, keepdims=True)
+        s_h[pl.ds(base, count), 0, :] = mm(e_of, dots * l_of, TN, highest)
+
+        def back(j, c):
+            cols = pl.ds(pl.multiple_of(j * 256, 256), 256)
+            grow[rows_m, cols] = mm(gh[rows_m, :], win[cols, :], NT).astype(bf16)
+            return c
+
+        lax.fori_loop(0, width // 256, back, 0)
+        s_gr[blk, :width] = grow[at : at + 8 * count]
+        tail = grow[at + 8 * count : at + m]
+        s_gr[blk, width:] = (
+            mm(p1, tail[:, :half_w], TN) + mm(p2, tail[:, half_w:], TN)
+        ).astype(bf16)
+        send_group(3, s_gr, r_gr, 8, group)
+        send_group(4, s_h, r_h, 0, group)
+
+    self_copy(3, s_gr, r_gr, 8).start()
+    self_copy(4, s_h, r_h, 0).start()
+    outs = [
+        pltpu.make_async_copy(xs, xs_hbm, out_sem.at[0]),
+        pltpu.make_async_copy(gos, gp_hbm, out_sem.at[1]),
+        pltpu.make_async_copy(act, act_hbm, out_sem.at[2]),
+        pltpu.make_async_copy(gh, gh_hbm, out_sem.at[3]),
+    ]
+    for c in outs:
+        c.start()
+
+    self_copy(3, s_gr, r_gr, 8).wait()
+
+    def down(j, c):
+        cols = pl.ds(pl.multiple_of(j * 256, 256), 256)
+        grow[:, cols] = mm(act[...], whid[:, cols]).astype(bf16)
+        return c
+
+    lax.fori_loop(0, width // 256, down, 0)
+    for base, count, which in order:
+        m = 12 * count
+        at = starts[which]
+        blk = pl.ds(pl.multiple_of(base * 8, 8 * count), 8 * count)
+        r4 = iota((4 * count, 8 * count), 0)
+        c8 = iota((4 * count, 8 * count), 1)
+        hit = (r4 // 4) == (c8 // 8)
+        p1 = jnp.where(hit & ((r4 % 4) == (c8 % 8)), 1.0, 0.0).astype(bf16)
+        p2 = jnp.where(hit & ((r4 % 4) + 4 == (c8 % 8)), 1.0, 0.0).astype(bf16)
+        s_pr[blk, :width] = grow[at : at + 8 * count]
+        tail = grow[at + 8 * count : at + m]
+        s_pr[blk, width:] = (
+            mm(p1, tail[:, :half_w], TN) + mm(p2, tail[:, half_w:], TN)
+        ).astype(bf16)
+        send_group(5, s_pr, r_pr, 8, (base, count, which))
+    self_copy(5, s_pr, r_pr, 8).start()
+
+    self_copy(4, s_h, r_h, 0).wait()
+    for group in order:
+        wait_group(4, s_h, r_h, 0, group)
+        wait_group(3, s_gr, r_gr, 8, group)
+    y_hat, y_r = hat(resid[...])
+    low = (y_hat * gain_moe[...] + shift_moe[...]).astype(bf16)
+    back_rows = r_h[:, 0, :]
+    dots = [jnp.sum(mm(hits[k], back_rows, NN, highest) * marks[k], axis=1, keepdims=True) for k in range(2)]
+    both = dots[0] + dots[1]
+    g_logits = ((dots[0] - gates[0] * both) * hits[0] + (dots[1] - gates[1] * both) * hits[1]).astype(bf16)
+    g_norm = collect(r_gr, None) + mm(g_logits, wr_ref[...], NT)
+    g_res = g_out[...] + norm_back(g_norm, y_hat, y_r, gain_moe[...])
+    gar[mine] = g_res.astype(bf16)
+    share = pair_copy(2, gar.at[mine], gar.at[mine])
+    share.start()
+    gin[...] = g_res
+    col_rows = mm(g_logits, low, TN)
+    moe_gain = jnp.sum(g_norm * y_hat, axis=0, keepdims=True)
+    moe_shift = jnp.sum(g_norm, axis=0, keepdims=True)
+    share.wait()
+
+    gmix[...] = mm(gar[...], wattn[...], NT).astype(bf16)
+    own_rows = HEAD_DIM // n_dp
+    n_loc = wl // HEAD_DIM
+    per = 2 * own_rows * n_loc
+    ci = iota((wl, n_dp * per), 1)
+    ri = iota((wl, n_dp * per), 0)
+    within = ci % per
+    row_r = (within // n_loc) % own_rows
+    want = (within % n_loc) * HEAD_DIM + (ci // per) * own_rows + row_r
+    pick = jnp.where(ri == want, 1.0, 0.0).astype(bf16)
+    mixed_p = mm(mixed[...], pick).astype(bf16)
+    block_shape = (2,) * 4 + (per, half_w)
+
+    def rs_put(t, val):
+        rsb[t] = val.astype(bf16).reshape(block_shape)
+
+    left = (iota((n_dp * per, half_w), 0) % per) < per // 2
+    rs_put(
+        3,
+        jnp.where(
+            left, mm(mixed_p, gar[:, :half_w], TN), mm(mixed_p, gar[:, half_w:], TN)
+        ),
+    )
+
+    bit_of = [lax.rem(dp // (1 << b), 2) for b in range(4)]
+    orders = ((0, 1, 2, 3), (1, 0, 2, 3), (2, 0, 1, 3), (1, 2, 0, 3))
+    stage_bufs = (rc0, rc1, rc2, rc3)
+
+    def rs_index(t, s, flip):
+        idx = [slice(None)] * 4
+        for b in orders[t][:s]:
+            idx[3 - b] = bit_of[b]
+        b = orders[t][s]
+        idx[3 - b] = 1 - bit_of[b] if flip else bit_of[b]
+        return (t, *idx)
+
+    def rs_copy(t, s):
+        b = orders[t][s]
+        partner = dp + (1 - 2 * bit_of[b]) * (1 << b)
+        return pltpu.make_async_remote_copy(
+            rsb.at[rs_index(t, s, True)],
+            stage_bufs[s].at[t],
+            rs_s.at[t, s],
+            rs_r.at[t, s],
+            device_id=(partner, hd),
+            device_id_type=MESH,
+        )
+
+    rs_copy(3, 0).start()
+
+    def attend_back(j, c):
+        cols = pl.ds(pl.multiple_of(j * 128, 128), 128)
+        q, k, v = qkv[0, :, cols], qkv[1, :, cols], qkv[2, :, cols]
+        gm = gmix[:, cols]
+        gq, gk, gv = [], [], []
+        for s in range(2):
+            p = probs[2 * j + s]
+            gpr = mm(jnp.where(lows[s], gm, jnp.zeros_like(gm)), v, NT)
+            ds = (p * (gpr - jnp.sum(p * gpr, axis=-1, keepdims=True))).astype(bf16)
+            gv.append(mm(p.astype(bf16), gm, TN))
+            gq.append(mm(ds, k) * scale)
+            gk.append(mm(ds, q, TN) * scale)
+        for t, g in enumerate((gq, gk, gv)):
+            gqkv[t, :, cols] = jnp.where(lows[0], g[0], g[1]).astype(bf16)
+        return c
+
+    lax.fori_loop(0, wl // 128, attend_back, 0)
+    for t in (2, 0, 1):
+        rs_put(t, mm(nr[...], gqkv[t], TN))
+        rs_copy(t, 0).start()
+
+    def to_rows(at):
+        return (
+            mm(gqkv[0, at, :], wqkv[0], NT)
+            + mm(gqkv[1, at, :], wqkv[1], NT)
+            + mm(gqkv[2, at, :], wqkv[2], NT)
+        )
+
+    npart[...] = to_rows(other).astype(bf16)
+    half_sum = pair_copy(3, npart, nrecv)
+    half_sum.start()
+    g_norm = to_rows(mine)
+    half_sum.wait()
+    g_norm = g_norm + nrecv[...].astype(f32)
+    x_hat, x_r = hat(x_in[...])
+    gin[...] = gin[...] + norm_back(g_norm, x_hat, x_r, gain_attn[...])
+    vec = jnp.concatenate(
+        [
+            col_rows,
+            jnp.sum(g_norm * x_hat, axis=0, keepdims=True),
+            jnp.sum(g_norm, axis=0, keepdims=True),
+            moe_gain,
+            moe_shift,
+            jnp.zeros((128 - experts - 4, width), f32),
+        ],
+        axis=0,
+    )
+    tall = vec.T.reshape(n, width // n // 8, 8, 128)
+    packed_small = tall[:, 0]
+    for j in range(1, width // n // 8):
+        packed_small = packed_small + pltpu.roll(tall[:, j].reshape(8 * n, 128), 40 * j, 1).reshape(n, 8, 128)
+    sm_s[...] = packed_small.reshape(8 * n, 128)
+    for group in order:
+        send_group(6, sm_s, sm_r, 8, group)
+    self_copy(6, sm_s, sm_r, 8).start()
+
+    for s in range(4):
+        for t in (3, 2, 0, 1):
+            rs_copy(t, s).wait()
+            at = rs_index(t, s, False)
+            total = rsb[at].astype(f32) + stage_bufs[s][t].astype(f32)
+            if s < 3:
+                rsb[at] = total.astype(bf16)
+                rs_copy(t, s + 1).start()
+            else:
+                rsf[t] = total
+
+    self_copy(5, s_pr, r_pr, 8).wait()
+    for group in order:
+        wait_group(5, s_pr, r_pr, 8, group)
+    lout[...] = resid[...] + (gates[0] * collect(r_pr, 0) + gates[1] * collect(r_pr, 1))
+    self_copy(6, sm_s, sm_r, 8).wait()
+    for group in order:
+        wait_group(6, sm_s, sm_r, 8, group)
+    small[...] = jnp.sum(sm_r[...].reshape(n, 8, 128), axis=0)
+    finals = [
+        pltpu.make_async_copy(lout, lout_hbm, out_sem.at[4]),
+        pltpu.make_async_copy(gin, gin_hbm, out_sem.at[5]),
+        pltpu.make_async_copy(rsf, rs_out_hbm, out_sem.at[6]),
+        pltpu.make_async_copy(small, small_hbm, out_sem.at[7]),
+    ]
+    for c in finals:
+        c.start()
+    for ph, s, d, u in (
+        (0, s_go, r_go, 8),
+        (1, s_x, r_x, 8),
+        (2, s_gt, r_gt, 0),
+        (3, s_gr, r_gr, 8),
+        (4, s_h, r_h, 0),
+        (5, s_pr, r_pr, 8),
+        (6, sm_s, sm_r, 8),
+    ):
+        drain(ph, s, d, u)
+    for c in outs + finals:
+        c.wait()
+
+
+def finish_kernel(
+    xs, gp, act, gh, frozen, lout_i, gin_i, rs_i, small_i, g_in, g_hid, lout, gin, gqkv, gattn, router, vecs
+):
+    train = (1 - frozen[0]).astype(f32)
+    g_in[0] = mm(xs[...], gh[...], TN) * train
+    g_hid[0] = mm(act[...], gp[...], TN) * train
+
+    @pl.when(pl.program_id(0) == 0)
+    def _():
+        lout[...] = lout_i[...]
+        gin[...] = gin_i[...]
+        for t in range(3):
+            gqkv[t] = rs_i[t]
+        n_loc = gattn.shape[0]
+        per, half_w = rs_i.shape[1:]
+        own_rows = per // 2 // n_loc
+        for r in range(own_rows):
+            for c in range(2):
+                first = (c * own_rows + r) * n_loc
+                gattn[:, (2 * r + c) * half_w : (2 * r + c + 1) * half_w] = rs_i[3, first : first + n_loc, :]
+        rows = router.shape[0]
+        parts = jnp.concatenate([small_i[:, 40 * j : 40 * j + 40] for j in range(rows // 8)], axis=0)
+        router[...] = parts[:, : router.shape[1]]
+        vecs[...] = parts[:, router.shape[1] :]
+
+
+def fast_body(
+    n_dp,
+    n_head,
+    layer_in,
+    grad_out,
+    w_qkv,
+    w_attn,
+    gain_attn,
+    shift_attn,
+    gain_moe,
+    shift_moe,
+    w_router,
+    w_in,
+    w_hidden,
+    expert_ids,
+    group_ids,
+    frozen,
+):
+    n = n_dp * n_head
+    rows, width = layer_in.shape
+    wl = w_attn.shape[0]
+    heads = wl // HEAD_DIM
+    experts = w_router.shape[1]
+    ff = w_in.shape[2]
+    length = rows * n_head
+    half_w = width // 2
+    packed = width + half_w
+    per = width // n_dp
+    pairs = 12 * n
+    sds = jax.ShapeDtypeStruct
+    any_space = pl.BlockSpec(memory_space=pl.ANY)
+    vmem = pl.BlockSpec(memory_space=pltpu.VMEM)
+    V = pltpu.VMEM
+    wide = V((8 * n, packed), bf16)
+    thin = V((n, 1, 128), f32)
+    dma = pltpu.SemaphoreType.DMA
+    out = pl.pallas_call(
+        functools.partial(layer_kernel, n_dp, n_head),
+        out_shape=(
+            sds((rows, width), f32),
+            sds((rows, width), f32),
+            sds((4, per, half_w), f32),
+            sds((8, 128), f32),
+            sds((pairs, width), bf16),
+            sds((pairs, width), bf16),
+            sds((pairs, ff), bf16),
+            sds((pairs, ff), bf16),
+        ),
+        in_specs=[any_space] * 4 + [vmem] * 5 + [any_space] * 2 + [vmem, pl.BlockSpec(memory_space=pltpu.SMEM)],
+        out_specs=(any_space,) * 8,
+        scratch_shapes=[
+            V((rows, width), f32),
+            V((rows, width), f32),
+            V((3, width, wl), bf16),
+            V((wl, width), bf16),
+            V((width, ff), bf16),
+            V((ff, width), bf16),
+            V((length, width), bf16),
+            V((3, length, wl), bf16),
+            V((heads, length, length), f32),
+            V((length, wl), bf16),
+            V((rows, width), f32),
+            V((rows, width), f32),
+            V((rows, width), f32),
+            V((2, rows, 8 * n), bf16),
+            V((2, rows, 8 * n), bf16),
+            V((2, rows, 8 * n), bf16),
+            wide,
+            wide,
+            wide,
+            wide,
+            thin,
+            thin,
+            wide,
+            wide,
+            thin,
+            thin,
+            wide,
+            wide,
+            V((pairs, width), bf16),
+            V((pairs, width), bf16),
+            V((pairs, ff), bf16),
+            V((pairs, ff), bf16),
+            V((pairs, width), bf16),
+            V((length, width), bf16),
+            V((length, wl), bf16),
+            V((3, length, wl), bf16),
+            V((rows, width), bf16),
+            V((rows, width), bf16),
+            V((4, 2, 2, 2, 2, per, half_w), bf16),
+            V((4, 2, 2, 2, per, half_w), bf16),
+            V((4, 2, 2, per, half_w), bf16),
+            V((4, 2, per, half_w), bf16),
+            V((4, per, half_w), bf16),
+            V((4, per, half_w), f32),
+            V((8 * n, 128), f32),
+            V((8 * n, 128), f32),
+            V((rows, width), f32),
+            V((rows, width), f32),
+            V((8, 128), f32),
+            dma((6,)),
+            dma((8,)),
+            dma((4,)),
+            dma((4,)),
+            dma((7, n)),
+            dma((7, n)),
+            dma((4, 4)),
+            dma((4, 4)),
+            dma((7,)),
+        ],
+        compiler_params=pltpu.CompilerParams(
+            collective_id=0, has_side_effects=True, vmem_limit_bytes=60 << 20
+        ),
+        name="layer",
+    )(
+        layer_in,
+        grad_out,
+        w_qkv,
+        w_attn,
+        gain_attn[None],
+        shift_attn[None],
+        gain_moe[None],
+        shift_moe[None],
+        w_router,
+        w_in,
+        w_hidden,
+        expert_ids,
+        group_ids,
+    )
+    lout, gin, rs, small, xs, gp, act, gh = out
+    fb = 256
+    whole = lambda *s: pl.BlockSpec(s, lambda j: (0,) * len(s))
+    res = pl.pallas_call(
+        finish_kernel,
+        grid=(ff // fb,),
+        out_shape=(
+            sds((1, width, ff), f32),
+            sds((1, ff, width), f32),
+            sds((rows, width), f32),
+            sds((rows, width), f32),
+            sds((3, per, wl), f32),
+            sds((heads, HEAD_DIM // n_dp * width), f32),
+            sds((width // n, experts), f32),
+            sds((width // n, 8), f32),
+        ),
+        in_specs=[
+            whole(pairs, width),
+            whole(pairs, width),
+            pl.BlockSpec((pairs, fb), lambda j: (0, j)),
+            pl.BlockSpec((pairs, fb), lambda j: (0, j)),
+            pl.BlockSpec(memory_space=pltpu.SMEM),
+            whole(rows, width),
+            whole(rows, width),
+            whole(4, per, half_w),
+            whole(8, 128),
+        ],
+        out_specs=(
+            pl.BlockSpec((1, width, fb), lambda j: (0, 0, j)),
+            pl.BlockSpec((1, fb, width), lambda j: (0, j, 0)),
+            whole(rows, width),
+            whole(rows, width),
+            whole(3, per, wl),
+            whole(heads, HEAD_DIM // n_dp * width),
+            whole(width // n, experts),
+            whole(width // n, 8),
+        ),
+        compiler_params=pltpu.CompilerParams(vmem_limit_bytes=48 << 20),
+        name="finish",
+    )(xs, gp, act, gh, frozen, lout, gin, rs, small)
+    g_in, g_hid, lout, gin, gqkv, gattn, router, vecs = res
+    return (lout, gin, gqkv, gattn, vecs[:, 0], vecs[:, 1], vecs[:, 2], vecs[:, 3], router, g_in, g_hid)
 
 
 def in_blocks(x, dim, size):
@@ -246,6 +1041,24 @@
     )
 
 
+def tiles(n_dp, n_head, args):
+    layer_in, w_attn, w_router = args[0], args[3], args[8]
+    rows, width = layer_in.shape
+    n = n_dp * n_head
+    experts = w_router.shape[1]
+    return (
+        n_dp == 16
+        and n_head == 2
+        and experts == n
+        and max(2, 3 * rows // experts) == 12
+        and rows == 128
+        and width % (8 * n) == 0
+        and (width // n // 8) * 40 <= 128
+        and experts + 4 <= 40
+        and w_attn.shape[0] == width // 2
+    )
+
+
 def solution(mesh):
     placed = (
         P(("dp", "head"), None),
@@ -263,8 +1076,15 @@
         P("dp"),
         P(("dp", "head")),
     )
+    n_dp, n_head = mesh.shape["dp"], mesh.shape["head"]
+
+    def chosen(*args):
+        if tiles(n_dp, n_head, args):
+            return fast_body(n_dp, n_head, *args)
+        return body(*args)
+
     return jax.shard_map(
-        body,
+        chosen,
         mesh=mesh,
         in_specs=placed,
         out_specs=(

time: 325 us -> 138 us (0.42)
  Pallas kernels: 0 us -> 119 us
  waiting for transfers between devices: 105 us -> 0 us
  matrix products: 73.2 us -> 0 us
  blocking collectives: 47.3 us -> 0 us
  starting transfers between devices: 27 us -> 0 us
  other arithmetic: 21.1 us -> 0 us
  local copies, waits for them, and re-layouts: 32.7 us -> 16.2 us
  between operations: 16.1 us -> 1.97 us
    pallas_call x0 -> x2, Pallas kernels: none -> 119 us  [the longest x1 105 us: fast_body(): pl.pallas_call(functools.partial(layer_kernel, n_dp, n_head), out_shape=(...]
    dot_general x25 -> x0, matrix products: 73.2 us -> none  [the longest x1 9.53 us: body(): jnp.einsum('sif,sid->fd', activated, grad_arrived, preferred_element_type...]
    all_to_all x6 -> x0, waiting for transfers between devices: 49.7 us -> none  [the longest x1 15.4 us: body(): lax.all_to_all(grad_rows, ('dp', 'head'), split_axis=0, concat_axis=0, ti...]
    unnamed x4 -> x0, waiting for transfers between devices: 47 us -> none
    unnamed x1 -> x0, blocking collectives: 43.1 us -> none
    all_to_all x6 -> x0, starting transfers between devices: 26.9 us -> none  [the longest x2 9.68 us: sum_at_owner(): lax.all_to_all(blocks, axis, split_axis=0, concat_axis=0, tiled=True)]
    reduce_sum x16 -> x0, other arithmetic: 13.6 us -> none  [the longest x2 4.36 us: sum_at_owner(): return arrived.astype(jnp.float32).sum(axis=0)]
    convert_element_type x6 -> x0, local copies, waits for them, and re-layouts: 10.7 us -> none  [the longest x2 4.48 us: body(): grad_w_attn.reshape(head_count, HEAD_DIM * width).astype(jnp.bfloat16)]
  transfers between devices with their start and end apart: 9 -> 0, of which waited for: 7 -> 0; matrix products, arithmetic and copies ran while one was open for 26% -> 0% of each run, Pallas kernels for 0% -> 0%
where the time goes in v1:
time: 138 us; the launch traced here: 137 us
  Pallas kernels  119 us (86%)
  local copies, waits for them, and re-layouts  16.2 us (12%)
  between operations  1.97 us (1%)
    pallas_call x1, Pallas kernels, fast_body(): pl.pallas_call(functools.partial(layer_kernel, n_dp, n_head), out_shape=(...  105 us
    pallas_call x1, Pallas kernels, fast_body(): pl.pallas_call(finish_kernel, grid=(ff // fb,), out_shape=(sds((1, width,...  13.8 us
    unnamed x16, local copies, waits for them, and re-layouts  10.4 us

profile of v1, /device:TPU:0, one launch (start us, length us, event | category | flops | bytes accessed | tf_op | source)
XLA Modules:
  0.0 137.4 jit_solution(3870088261880811040)
XLA Ops:
  1.9 1.3 broadcast_in_dim.12.gain_attn
  3.2 1.3 broadcast_in_dim.13.shift_attn
  4.5 1.3 broadcast_in_dim.14.gain_moe
  5.7 1.3 broadcast_in_dim.15.shift_moe
  7.0 1.4 %copy.28.ids_ref = s32[128,2]{1,0:T(8,128)} copy(s32[128,2]{0,1:T(2,128)} %param.25) | data formatting | bytes 2048 | tf_op args[11]
  8.4 1.6 %copy.27.wr_ref = bf16[768,32]{1,0:T(8,128)(2,1)} copy(bf16[768,32]{0,1:T(8,128)(2,1)} %param.22) | data formatting | bytes 98304 | tf_op args[8]
  10.0 105.4 %layer.1 = (f32[128,768]{1,0:T(8,128)}, f32[128,768]{1,0:T(8,128)}, f32[4,48,384]{2,1,0:T(8,128)}, f32[8,128]{1,0:T(8,128)}, bf16[384,768]{1,0:T(8,128)(2,1)}, /...) custom-call(f32[128,768]{1,0:T(8,128)} %in_hbm.1, f32[128,768]{1,0:T(8,128)} %gout_hbm.1, ...), custom_call_target="tpu_custom_call" | custom-call | tf_op jit(solution)/shard_map/layer/pallas_call | solution.py:671
  115.4 0.0 copy-start
  115.4 1.7 %copy-done = bf16[384,3072]{1,0:T(8,128)(2,1)S(1)} copy-done((bf16[384,3072]{1,0:T(8,128)(2,1)S(1)}, bf16[384,3072]{1,0:T(8,128)(2,1)}, u32[]{:S(2)}) %copy-start) | copy-done | bytes 2359320
  117.1 0.0 copy-start.1
  117.1 1.1 copy-done.1
  118.2 0.0 copy-start.2
  118.2 1.1 copy-done.2
  119.2 0.0 copy-start.3
  119.2 1.0 copy-done.3
  120.2 0.0 copy-start.4
  120.2 1.0 copy-done.4
  121.2 0.0 copy-start.5
  121.2 1.0 copy-done.5
  122.2 0.0 copy-start.6
  122.2 0.7 copy-done.6
  122.9 13.8 %finish.1 = (f32[1,768,3072]{2,1,0:T(8,128)}, f32[1,3072,768]{2,1,0:T(8,128)}, f32[128,768]{1,0:T(8,128)}, f32[128,768]{1,0:T(8,128)}, f32[3,48,384]{2,1,0:T(8,1...) custom-call(bf16[384,768]{1,0:T(8,128)(2,1)S(1)} %copy-done.1, bf16[384,768]{1,0:T(8,128)(2,1)S(1)} %copy-done.2, ...), custom_call_target="tpu_custom_call" | custom-call | tf_op jit(solution)/shard_map/finish/pallas_call | solution.py:767
  136.7 0.7 slice_reduce_fusion
Async XLA Ops:
  115.4 1.7 %copy-start = (bf16[384,3072]{1,0:T(8,128)(2,1)S(1)}, bf16[384,3072]{1,0:T(8,128)(2,1)}, u32[]{:S(2)}) copy-start(bf16[384,3072]{1,0:T(8,128)(2,1)} %get-tuple-element.29.act) | copy-start | bytes 7077892
  117.1 1.1 copy-start.1
  118.2 1.1 copy-start.2
  119.2 1.0 copy-start.3
  120.2 1.0 copy-start.4
  121.2 1.0 copy-start.5
  122.2 0.7 copy-start.6
